TPU v7x, 32 devices: a whole 2x2x4 slice. The times are simulated.
32 devices in a mesh: feat: 4 (over y, x), label: 8 (over z, core).
Axes of the slice: x: 2, y: 2, z: 4, core: 2. Of those that a mesh axis runs over, the one named last changes fastest.
Arguments:
- documents: bfloat16 [160, 1024], P(None, 'label'), may hold values from -6 to 6
- expand_weight: bfloat16 [1024, 32768], P('label', 'feat'), may hold values from -0.1875 to 0.1875
- sparse_weight: bfloat16 [768, 16, 128, 128], P(('feat', 'label')), may hold values from -0.125 to 0.125
- feature_lists: int32 [768, 16], replicated, may hold values from 0 to 255, as said below
- positives: int32 [160, 8], replicated, may hold values from 0 to 98303
Outputs:
- grad_expand: bfloat16 [1024, 32768], P('label', 'feat')
- grad_sparse: bfloat16 [768, 16, 128, 128], P(('feat', 'label'))
Inputs may be any that keep to these rules, and one draw needn't show every extreme that they name: `feature_lists`: within each aligned group of 24 label blocks (taken in order), the entries name exactly 24 distinct feature blocks from each range of 64 consecutive blocks, each named exactly 4 times in the group; the 16 entries of one label block are distinct.
All inputs are finite; a program needn't handle non-finite values.
Results may differ from a plain program's by a relative error of at most 0.014.
Values may be sent and summed in bfloat16 or wider, within the bound.
No kernel may reach another device: no remote copies, remote signals or barrier semaphores. Data moves between devices by JAX's collectives and lax.ppermute only.
A program may use at most 192 MiB of HBM per device.

v0:
```python
import jax
import jax.numpy as jnp
from jax import lax
from jax.sharding import PartitionSpec as P

BLK = 128
FBLOCKS = 256
SLOTS = 16
LBLK_DEV = 24
CAP = 24


def on_device(documents, expand_weight, sparse_weight, feature_lists, positives):
    feat_count = lax.axis_size("feat")
    label_count = lax.axis_size("label")
    feat_index = lax.axis_index("feat")
    label_index = lax.axis_index("label")
    group = feat_index * label_count + label_index
    doc_count = documents.shape[0]
    width_local = expand_weight.shape[0]
    own_count = expand_weight.shape[1] // BLK
    local_weight = expand_weight.reshape(width_local, own_count, BLK)
    partial_pre = jnp.einsum(
        "dk,kbc->bdc", documents, local_weight, preferred_element_type=jnp.float32
    )
    summed_pre = lax.psum(partial_pre, "label")
    hidden = jnp.maximum(summed_pre, 0.0).astype(jnp.bfloat16)
    mine = lax.dynamic_slice_in_dim(feature_lists, group * LBLK_DEV, LBLK_DEV, 0)

    def sender_list(target):
        rows = lax.dynamic_slice_in_dim(
            feature_lists, (target * label_count + label_index) * LBLK_DEV, LBLK_DEV, 0
        )
        local_ids = feat_index * own_count + jnp.arange(own_count, dtype=jnp.int32)
        used = jnp.any(rows.reshape(-1)[:, None] == local_ids[None, :], axis=0)
        order = jnp.argsort(jnp.where(used, 0, 1).astype(jnp.int32), stable=True)
        return order[:CAP]

    send_index = jax.vmap(sender_list)(jnp.arange(feat_count, dtype=jnp.int32))
    outgoing = jnp.take(hidden, send_index, axis=0)
    incoming = lax.all_to_all(outgoing, "feat", split_axis=0, concat_axis=0, tiled=True)
    present = jnp.any(
        mine.reshape(-1)[:, None] == jnp.arange(FBLOCKS, dtype=jnp.int32)[None, :], axis=0
    )
    ranks = jnp.cumsum(present.reshape(feat_count, own_count).astype(jnp.int32), axis=1) - 1
    position_table = (jnp.arange(feat_count, dtype=jnp.int32)[:, None] * CAP + ranks).reshape(-1)
    slot_position = jnp.take(position_table, mine, axis=0)
    picked = jnp.take(incoming.reshape(feat_count * CAP, doc_count, BLK), slot_position, axis=0)
    logits = jnp.einsum("lsdc,lsce->dle", picked, sparse_weight, preferred_element_type=jnp.float32)
    label_ids = (group * LBLK_DEV + jnp.arange(LBLK_DEV, dtype=jnp.int32))[
        :, None
    ] * BLK + jnp.arange(BLK, dtype=jnp.int32)[None, :]
    targets = jnp.any(positives[:, :, None, None] == label_ids[None, None, :, :], axis=1).astype(
        jnp.float32
    )
    residual = (jax.nn.sigmoid(logits) - targets).astype(jnp.bfloat16)
    grad_sparse = jnp.einsum(
        "lsdc,dle->lsce", picked, residual, preferred_element_type=jnp.float32
    ).astype(jnp.bfloat16)
    back = jnp.einsum("dle,lsce->lsdc", residual, sparse_weight, preferred_element_type=jnp.float32)
    back_rows = back.reshape(LBLK_DEV * SLOTS, doc_count, BLK)
    group_part = jax.ops.segment_sum(
        back_rows, slot_position.reshape(-1), num_segments=feat_count * CAP
    )
    group_part = group_part.astype(jnp.bfloat16).reshape(feat_count, CAP, doc_count, BLK)
    returned = lax.all_to_all(group_part, "feat", split_axis=0, concat_axis=0, tiled=True)
    column_sum = jax.ops.segment_sum(
        returned.astype(jnp.float32).reshape(feat_count * CAP, doc_count, BLK),
        send_index.reshape(-1),
        num_segments=own_count,
    )
    block_grad = lax.psum(column_sum.astype(jnp.bfloat16), "label").astype(jnp.float32)
    grad_hidden = jnp.where(hidden > 0, block_grad, 0.0).astype(jnp.bfloat16)
    grad_expand = jnp.einsum(
        "dk,bdc->kbc", documents, grad_hidden, preferred_element_type=jnp.float32
    )
    grad_expand = grad_expand.reshape(width_local, own_count * BLK).astype(jnp.bfloat16)
    return (grad_expand, grad_sparse)


def solution(mesh):
    return jax.shard_map(
        on_device,
        mesh=mesh,
        in_specs=(
            P(None, "label"),
            P("label", "feat"),
            P(("feat", "label"), None, None, None),
            P(),
            P(),
        ),
        out_specs=(P("label", "feat"), P(("feat", "label"), None, None, None)),
        check_vma=False,
    )
```

profile of v0, /device:TPU:0, one launch (start us, length us, event | category | flops | bytes accessed | tf_op | source)
XLA Modules:
  0.0 502.6 jit_solution(14127657274373574968)
XLA Ops:
  7.2 8.1 %while.1 = (s32[]{:T(128)}, s32[768,16]{0,1:T(8,128)}, s32[4,2]{0,1:T(2,128)S(1)}, s32[4,24,16]{1,2,0:T(8,128)S(1)}, s32[]{:T(128)}) while((s32[]{:T(128)}, s32[768,16]{0,1:T(8,128)}, s32[4,2]{0,1:T(2,128)S(1)}, s32[4,24,16]{1,2,0:T(8,128)S(1)}, s32[]{:T(128)}) %tuple.25), condition=%wide.while_cond, body=%wide.while_body.sunk | while | flops 2 | bytes 9825 | solution.py:31
  7.2 0.1 constant_dynamic-slice_fusion.3
  7.3 0.5 slice.26
  7.8 1.4 bitcast_dynamic-update-slice_fusion.2
  9.3 0.1 constant_dynamic-slice_fusion.3
  9.3 0.5 slice.26
  9.9 1.4 bitcast_dynamic-update-slice_fusion.2
  11.3 0.1 constant_dynamic-slice_fusion.3
  11.4 0.5 slice.26
  11.9 1.4 bitcast_dynamic-update-slice_fusion.2
  13.3 0.1 constant_dynamic-slice_fusion.3
  13.4 0.5 slice.26
  13.9 1.4 bitcast_dynamic-update-slice_fusion.2
  15.4 0.1 copy.20
  15.4 0.1 eq.43
  15.5 0.2 compare_reduce_fusion.1
  15.8 0.1 copy.21
  15.9 1.0 sort.17
  16.9 0.1 copy.25
  17.0 0.1 reshape.170
  17.1 4.0 convolution_bitcast_fusion
  21.1 111.1 %all-reduce.5 = bf16[64,160,128]{2,1,0:T(8,128)(2,1)} all-reduce(f32[64,160,128]{2,1,0:T(8,128)} %convolution_bitcast_fusion), channel_id=1, replica_groups=mesh['feat'=4,'label'=8] {'label'}, use_global_device_ids=true, to_apply=%region_0.0 | all-reduce | flops 1310720 | bytes 7864320 | tf_op jit(solution)/shard_map/psum | solution.py:26
  132.1 3.8 maximum_convert_fusion
  135.9 0.1 copy.24
  136.0 4.8 gather_fusion.1
  140.8 4.5 broadcast_select_fusion.5
  145.3 5.0 all-to-all-start
  150.3 0.8 constant_dynamic-slice_fusion.1
  151.1 0.1 copy.31
  151.2 0.1 eq.47
  151.2 0.1 reshape.162
  151.3 0.1 fusion.16
  151.5 0.1 reshape.157
  151.6 0.2 reduce_window_sum.11
  151.8 0.1 add_add_fusion
  151.9 0.1 add.134
  152.0 2.8 gather_fusion
  154.8 0.1 reshape.161
  154.9 0.1 reshape.186
  155.0 0.1 reshape.178
  155.1 0.1 copy.26
  155.2 0.1 iota_add_fusion
  155.3 3.7 compare_reduce_fusion
  159.0 32.3 %all-to-all-done = bf16[4,24,160,128]{3,2,1,0:T(8,128)(2,1)} async-done(((bf16[4,24,160,128]{3,2,1,0:T(8,128)(2,1)}), bf16[4,24,160,128]{3,2,1,0:T(8,128)(2,1)}, u32[]{:S(2)}, u32[]{:S(2)}) %all-to-all-start) | async-done | bytes 3932192 | tf_op jit(solution)/shard_map/all_to_all | solution.py:41
  191.3 14.7 %gather_fusion.2 = bf16[384,160,128]{2,1,0:T(8,128)(2,1)} fusion(bf16[96,160,128]{2,1,0:T(8,128)(2,1)} %bitcast.3, s32[1024]{0:T(1024)S(1)} %pad_clamp_fusion), kind=kCustom, calls=%fused_computation.2 | custom fusion | bytes 31458816 | tf_op jit(solution)/shard_map/jit(_take)/gather | solution.py:48
  206.0 11.4 %fusion.14 = bf16[160,24,128,1]{2,0,3,1:T(8,128)(2,1)S(1)} fusion(pred[160,24,128]{2,1,0:T(8,128)(4,1)S(1)} %compare_reduce_fusion, bf16[24,16,128,128]{3,2,1,0:T(8,128)(2,1)} %param.7, bf16[24,16,160,128]{3,2,1,0:T(8,128)(2,1)} %bitcast.62, pred[24,16]{1,0:T(8,128)(4,1)S(1)} %get-tuple-element.26), kind=kOutput, calls=%fused_computation.30 | convolution fusion | flops 2024079360 | bytes 29786496 | tf_op jit(solution)/shard_map/lsdc,lsce->dle/dot_general | solution.py:49
  217.4 15.2 %fusion.23 = f32[24,160,16,128]{3,1,2,0:T(8,128)} fusion(bf16[160,24,128,1]{2,0,3,1:T(8,128)(2,1)S(1)} %fusion.14, bf16[24,16,128,128]{3,2,1,0:T(8,128)(2,1)} %param.7), kind=kOutput, calls=%fused_computation.58 | convolution fusion | flops 2013265920 | bytes 45023232 | tf_op jit(solution)/shard_map/dle,lsce->lsdc/dot_general | solution.py:60
  232.6 4.2 broadcast_in_dim.58
  236.8 87.4 %scatter_fusion = f32[96,160,128]{2,1,0:T(8,128)} fusion(f32[96,160,128]{2,1,0:T(8,128)} %broadcast_in_dim.58, s32[384]{0:T(512)S(1)} %reshape.186, f32[384,160,128]{2,1,0:T(8,128)} %bitcast.61), kind=kCustom, calls=%fused_computation.3 | custom fusion | flops 7864320 | bytes 94373376 | tf_op jit(solution)/shard_map/scatter-add | solution.py:62
  324.3 5.8 %convert_element_type.45 = bf16[96,160,128]{2,1,0:T(8,128)(2,1)} convert(f32[96,160,128]{2,1,0:T(8,128)} %scatter_fusion) | non-fusion elementwise | flops 1966080 | bytes 11796480 | tf_op jit(solution)/shard_map/convert_element_type | solution.py:65
  330.1 4.8 all-to-all-start.1
  334.9 0.3 all-reduce.4.cloned.1.call-start
  335.2 0.1 copy.22
  335.3 0.1 reshape.194
  335.4 43.7 %all-to-all-done.1 = bf16[4,24,160,128]{3,2,1,0:T(8,128)(2,1)} async-done(((bf16[4,24,160,128]{3,2,1,0:T(8,128)(2,1)}), bf16[4,24,160,128]{3,2,1,0:T(8,128)(2,1)}, u32[]{:S(2)}, u32[]{:S(2)}) %all-to-all-start.1) | async-done | bytes 3932192 | tf_op jit(solution)/shard_map/all_to_all | solution.py:66
  379.1 6.4 %bitcast_convert_fusion = f32[96,160,128]{2,1,0:T(8,128)} fusion(bf16[4,24,160,128]{3,2,1,0:T(8,128)(2,1)} %all-to-all-done.1), kind=kLoop, calls=%fused_computation.16 | loop fusion | flops 1966080 | bytes 11796480 | tf_op jit(solution)/shard_map/reshape | solution.py:68
  385.5 3.0 broadcast.134
  388.4 22.5 %scatter_fusion.1 = f32[64,160,128]{2,1,0:T(8,128)} fusion(f32[64,160,128]{2,1,0:T(8,128)} %broadcast.134, s32[96]{0:T(128)S(1)} %reshape.194, f32[96,160,128]{2,1,0:T(8,128)} %bitcast_convert_fusion), kind=kCustom, calls=%fused_computation.4 | custom fusion | flops 1966080 | bytes 23593344 | tf_op jit(solution)/shard_map/scatter-add | solution.py:67
  411.0 4.4 convert_element_type.46
  415.3 0.0 all-reduce.4.cloned.1.call-update
  415.4 14.3 %fusion.4 = bf16[24,16,128,128]{3,2,1,0:T(8,128)(2,1)} fusion(bf16[160,24,128,1]{2,0,3,1:T(8,128)(2,1)S(1)} %fusion.14, bf16[24,16,160,128]{3,2,1,0:T(8,128)(2,1)} %bitcast.63, pred[24,16]{1,0:T(8,128)(4,1)S(1)} %get-tuple-element.26), kind=kOutput, calls=%fused_computation.13 | convolution fusion | flops 2027421696 | bytes 29294976 | tf_op jit(solution)/shard_map/lsdc,dle->lsce/dot_general | solution.py:57
  429.6 56.8 %all-reduce.4.cloned.1.call-done = bf16[64,160,128]{2,1,0:T(8,128)(2,1)} async-done(((bf16[64,160,128]{2,1,0:T(8,128)(2,1)}), bf16[64,160,128]{2,1,0:T(8,128)(2,1)}) %all-reduce.4.cloned.1.call-update) | async-done | bytes 2621456 | tf_op jit(solution)/shard_map/psum | solution.py:72
  486.5 5.2 %fusion.13 = bf16[64,128,128]{2,1,0:T(8,128)(2,1)} fusion(bf16[64,160,128]{2,1,0:T(8,128)(2,1)} %all-reduce.4.cloned.1.call-done, bf16[160,128]{1,0:T(8,128)(2,1)S(1)} %copy-done.2, bf16[64,160,128]{2,1,0:T(8,128)(2,1)} %all-reduce.5), kind=kOutput, calls=%fused_computation.29 | convolution fusion | flops 345767936 | bytes 7380992 | tf_op jit(solution)/shard_map/dk,bdc->kbc/dot_general | solution.py:74
  491.6 4.1 copy.28
  (25 shorter events, 0.1 us)
Async XLA Ops:
  7.2 9.9 %copy-start = (bf16[128,8192]{1,0:T(8,128)(2,1)S(1)}, bf16[128,8192]{1,0:T(8,128)(2,1)}, u32[]{:S(2)}) copy-start(bf16[128,8192]{1,0:T(8,128)(2,1)} %param.6) | copy-start | bytes 6291460
  145.3 46.0 %all-to-all-start = ((bf16[4,24,160,128]{3,2,1,0:T(8,128)(2,1)}), bf16[4,24,160,128]{3,2,1,0:T(8,128)(2,1)}, u32[]{:S(2)}, u32[]{:S(2)}) async-start(bf16[4,24,160,128]{3,2,1,0:T(8,128)(2,1)} %broadcast_select_fusion.5), calls=%async_computation | async-start | bytes 7864320 | tf_op jit(solution)/shard_map/all_to_all | solution.py:41
  152.0 3.1 copy-start.3
  330.1 48.9 %all-to-all-start.1 = ((bf16[4,24,160,128]{3,2,1,0:T(8,128)(2,1)}), bf16[4,24,160,128]{3,2,1,0:T(8,128)(2,1)}, u32[]{:S(2)}, u32[]{:S(2)}) async-start(bf16[4,24,160,128]{3,2,1,0:T(8,128)(2,1)} %bitcast.64), calls=%async_computation.1 | async-start | bytes 7864320 | tf_op jit(solution)/shard_map/all_to_all | solution.py:66
  334.9 151.5 %all-reduce.4.cloned.1.call-start = ((), (), s32[]{:S(2)}) async-start(), calls=%async_computation.2 | async-start | bytes 5242880 | tf_op jit(solution)/shard_map/psum | solution.py:72
  415.3 71.1 %copy-start.2 = (bf16[160,128]{1,0:T(8,128)(2,1)S(1)}, bf16[160,128]{1,0:T(8,128)(2,1)}, u32[]{:S(2)}) copy-start(bf16[160,128]{1,0:T(8,128)(2,1)} %param.5) | copy-start | bytes 122884
  415.4 80.4 %copy-start.1 = (bf16[128,8192]{1,0:T(8,128)(2,1)S(1)}, bf16[128,8192]{1,0:T(8,128)(2,1)}, u32[]{:S(2)}) copy-start(bf16[128,8192]{1,0:T(8,128)(2,1)} %param.6) | copy-start | bytes 6291460
Sparse Core Ops, SparseCore 0:
  415.5 70.9 all-reduce.3
where the time goes:
time: 505 us; the launch traced here: 503 us
  other arithmetic  140 us (28%)
  waiting for transfers between devices  133 us (26%)
  blocking collectives  111 us (22%)
  matrix products  50.1 us (10%)
  local copies, waits for them, and re-layouts  44 us (9%)
  between operations  14.2 us (3%)
  starting transfers between devices  10 us (2%)
    psum x1, blocking collectives, on_device(): summed_pre = lax.psum(partial_pre, 'label')  111 us
    scatter-add x1, other arithmetic, on_device(): jax.ops.segment_sum(back_rows, slot_position.reshape(-1), num_segments=fe...  87.4 us
    psum x1, waiting for transfers between devices, on_device(): lax.psum(column_sum.astype(jnp.bfloat16), 'label').astype(jnp.float32)  56.8 us
    all_to_all x1, waiting for transfers between devices, on_device(): lax.all_to_all(group_part, 'feat', split_axis=0, concat_axis=0, tiled=True)  43.7 us
    all_to_all x1, waiting for transfers between devices, on_device(): lax.all_to_all(outgoing, 'feat', split_axis=0, concat_axis=0, tiled=True)  32.3 us
    scatter-add x1, other arithmetic, on_device(): jax.ops.segment_sum(returned.astype(jnp.float32).reshape(feat_count * CAP...  22.5 us
    dot_general x1, matrix products, on_device(): jnp.einsum('dle,lsce->lsdc', residual, sparse_weight, preferred_element_t...  15.2 us
    gather x1, local copies, waits for them, and re-layouts, on_device(): jnp.take(incoming.reshape(feat_count * CAP, doc_count, BLK), slot_positio...  14.7 us
  transfers between devices with their start and end apart: 3, of which 3 were waited for; matrix products, arithmetic and copies ran while one was open for 5% of the time, Pallas kernels for 0%

commit v1 on v0

--- a/solution.py
+++ b/solution.py
@@ -11,6 +11,10 @@
 
 
 def on_device(documents, expand_weight, sparse_weight, feature_lists, positives):
+
+    def end_tails(frame_in, axis_key):
+        return lax.all_gather(frame_in, axis_key).sum(axis=0)
+
     feat_count = lax.axis_size("feat")
     label_count = lax.axis_size("label")
     feat_index = lax.axis_index("feat")
@@ -23,7 +27,7 @@
     partial_pre = jnp.einsum(
         "dk,kbc->bdc", documents, local_weight, preferred_element_type=jnp.float32
     )
-    summed_pre = lax.psum(partial_pre, "label")
+    summed_pre = end_tails(partial_pre, "label")
     hidden = jnp.maximum(summed_pre, 0.0).astype(jnp.bfloat16)
     mine = lax.dynamic_slice_in_dim(feature_lists, group * LBLK_DEV, LBLK_DEV, 0)
 

time: 505 us -> 765 us (1.51)
  waiting for transfers between devices: 133 us -> 485 us
  blocking collectives: 111 us -> 0 us
  other arithmetic: 140 us -> 158 us
    all_gather x0 -> x1, waiting for transfers between devices: none -> 352 us  [end_tails(): return lax.all_gather(frame_in, axis_key).sum(axis=0)]
    psum x1 -> x0, blocking collectives: 111 us -> none  [on_device(): summed_pre = lax.psum(partial_pre, 'label')]
    reduce_sum x0 -> x1, other arithmetic: none -> 18 us  [end_tails(): return lax.all_gather(frame_in, axis_key).sum(axis=0)]
  transfers between devices with their start and end apart: 3 -> 4, of which waited for: 3 -> 4; matrix products, arithmetic and copies ran while one was open for 5% -> 4% of each run, Pallas kernels for 0% -> 0%
where the time goes in v1:
time: 765 us; the launch traced here: 763 us
  waiting for transfers between devices  485 us (63%)
  other arithmetic  158 us (21%)
  matrix products  50.2 us (7%)
  local copies, waits for them, and re-layouts  45 us (6%)
  between operations  14.2 us (2%)
  starting transfers between devices  10.1 us (1%)
    all_gather x1, waiting for transfers between devices, end_tails(): return lax.all_gather(frame_in, axis_key).sum(axis=0)  352 us
    scatter-add x1, other arithmetic, on_device(): jax.ops.segment_sum(back_rows, slot_position.reshape(-1), num_segments=fe...  87.4 us
    psum x1, waiting for transfers between devices, on_device(): lax.psum(column_sum.astype(jnp.bfloat16), 'label').astype(jnp.float32)  52.6 us
    all_to_all x1, waiting for transfers between devices, on_device(): lax.all_to_all(group_part, 'feat', split_axis=0, concat_axis=0, tiled=True)  44 us
    all_to_all x1, waiting for transfers between devices, on_device(): lax.all_to_all(outgoing, 'feat', split_axis=0, concat_axis=0, tiled=True)  36.4 us
    scatter-add x1, other arithmetic, on_device(): jax.ops.segment_sum(returned.astype(jnp.float32).reshape(feat_count * CAP...  22.5 us
    reduce_sum x1, other arithmetic, end_tails(): return lax.all_gather(frame_in, axis_key).sum(axis=0)  18 us
  transfers between devices with their start and end apart: 4, of which 4 were waited for; matrix products, arithmetic and copies ran while one was open for 4% of the time, Pallas kernels for 0%

profile of v1, /device:TPU:0, one launch (start us, length us, event | category | flops | bytes accessed | tf_op | source)
XLA Modules:
  0.0 763.1 jit_solution(13063993140037701146)
XLA Ops:
  7.2 1.5 copy-done
  8.8 4.0 convolution_bitcast_fusion
  12.8 7.6 while.1
  12.8 0.1 constant_dynamic-slice_fusion.3
  12.9 0.5 slice.26
  13.4 1.3 bitcast_dynamic-update-slice_fusion.2
  14.7 0.1 constant_dynamic-slice_fusion.3
  14.8 0.5 slice.26
  15.3 1.3 bitcast_dynamic-update-slice_fusion.2
  16.6 0.1 constant_dynamic-slice_fusion.3
  16.7 0.5 slice.26
  17.2 1.3 bitcast_dynamic-update-slice_fusion.2
  18.5 0.1 constant_dynamic-slice_fusion.3
  18.6 0.5 slice.26
  19.1 1.3 bitcast_dynamic-update-slice_fusion.2
  20.4 0.1 copy.28
  20.5 0.1 eq.43
  20.6 0.2 compare_reduce_fusion.1
  20.8 0.1 copy.29
  21.0 1.0 sort.17
  22.0 0.1 copy.33
  22.1 0.1 reshape.170
  22.2 0.1 copy.32
  22.3 352.2 %all-gather.3.cloned.1.call-done = f32[512,160,128]{2,1,0:T(8,128)} async-done(((f32[64,160,128]{2,1,0:T(8,128)}), f32[512,160,128]{2,1,0:T(8,128)}) %all-gather.3.cloned.1.call-update) | async-done | bytes 41943056 | tf_op jit(solution)/shard_map/all_gather | solution.py:16
  374.5 18.0 %reduce_sum.9 = bf16[64,160,128]{2,1,0:T(8,128)(2,1)} reduce(f32[8,64,160,128]{3,2,1,0:T(8,128)} %bitcast.63, f32[]{:T(128)} %constant.24.clone.1), dimensions={0}, to_apply=%region_0.0 | reduce | flops 9175040 | bytes 44564484 | tf_op jit(solution)/shard_map/reduce_sum | solution.py:16
  392.5 3.8 maximum_convert_fusion
  396.2 4.8 gather_fusion.1
  401.1 4.5 broadcast_select_fusion.5
  405.5 5.0 all-to-all-start
  410.5 0.8 constant_dynamic-slice_fusion.1
  411.3 0.1 copy.39
  411.4 0.1 eq.47
  411.5 0.1 reshape.162
  411.6 0.1 fusion.16
  411.7 0.1 reshape.157
  411.8 0.2 reduce_window_sum.11
  412.1 0.1 add_add_fusion
  412.1 0.1 add.132
  412.2 2.8 gather_fusion
  415.0 0.1 reshape.161
  415.1 0.1 reshape.186
  415.2 0.1 reshape.178
  415.3 0.1 copy.34
  415.5 3.7 compare_reduce_fusion
  419.2 36.4 %all-to-all-done = bf16[4,24,160,128]{3,2,1,0:T(8,128)(2,1)} async-done(((bf16[4,24,160,128]{3,2,1,0:T(8,128)(2,1)}), bf16[4,24,160,128]{3,2,1,0:T(8,128)(2,1)}, u32[]{:S(2)}, u32[]{:S(2)}) %all-to-all-start) | async-done | bytes 3932192 | tf_op jit(solution)/shard_map/all_to_all | solution.py:45
  455.6 14.7 %gather_fusion.2 = bf16[384,160,128]{2,1,0:T(8,128)(2,1)} fusion(bf16[96,160,128]{2,1,0:T(8,128)(2,1)} %bitcast.4, s32[1024]{0:T(1024)S(1)} %pad_clamp_fusion), kind=kCustom, calls=%fused_computation.2 | custom fusion | bytes 31458816 | tf_op jit(solution)/shard_map/jit(_take)/gather | solution.py:52
  470.4 11.4 %fusion.14 = bf16[160,24,128,1]{2,0,3,1:T(8,128)(2,1)S(1)} fusion(pred[160,24,128]{2,1,0:T(8,128)(4,1)S(1)} %compare_reduce_fusion, bf16[24,16,128,128]{3,2,1,0:T(8,128)(2,1)} %param.7, bf16[24,16,160,128]{3,2,1,0:T(8,128)(2,1)} %bitcast.64, pred[24,16]{1,0:T(8,128)(4,1)S(1)} %get-tuple-element.28), kind=kOutput, calls=%fused_computation.30 | convolution fusion | flops 2024079360 | bytes 29786496 | tf_op jit(solution)/shard_map/lsdc,lsce->dle/dot_general | solution.py:53
  481.8 15.2 %fusion.23 = f32[24,160,16,128]{3,1,2,0:T(8,128)} fusion(bf16[160,24,128,1]{2,0,3,1:T(8,128)(2,1)S(1)} %fusion.14, bf16[24,16,128,128]{3,2,1,0:T(8,128)(2,1)} %param.7), kind=kOutput, calls=%fused_computation.58 | convolution fusion | flops 2013265920 | bytes 45023232 | tf_op jit(solution)/shard_map/dle,lsce->lsdc/dot_general | solution.py:64
  497.0 4.2 broadcast_in_dim.58
  501.2 87.4 %scatter_fusion = f32[96,160,128]{2,1,0:T(8,128)} fusion(f32[96,160,128]{2,1,0:T(8,128)} %broadcast_in_dim.58, s32[384]{0:T(512)S(1)} %reshape.186, f32[384,160,128]{2,1,0:T(8,128)} %bitcast.62), kind=kCustom, calls=%fused_computation.3 | custom fusion | flops 7864320 | bytes 94373376 | tf_op jit(solution)/shard_map/scatter-add | solution.py:66
  588.6 5.8 convert_element_type.45
  594.5 4.8 all-to-all-start.1
  599.3 0.3 all-reduce.3.cloned.1.call-start
  599.6 0.1 copy.30
  599.6 0.1 reshape.194
  599.7 44.0 %all-to-all-done.1 = bf16[4,24,160,128]{3,2,1,0:T(8,128)(2,1)} async-done(((bf16[4,24,160,128]{3,2,1,0:T(8,128)(2,1)}), bf16[4,24,160,128]{3,2,1,0:T(8,128)(2,1)}, u32[]{:S(2)}, u32[]{:S(2)}) %all-to-all-start.1) | async-done | bytes 3932192 | tf_op jit(solution)/shard_map/all_to_all | solution.py:70
  643.8 6.4 bitcast_convert_fusion
  650.2 3.0 broadcast.134
  653.1 22.5 %scatter_fusion.1 = f32[64,160,128]{2,1,0:T(8,128)} fusion(f32[64,160,128]{2,1,0:T(8,128)} %broadcast.134, s32[96]{0:T(128)S(1)} %reshape.194, f32[96,160,128]{2,1,0:T(8,128)} %bitcast_convert_fusion), kind=kCustom, calls=%fused_computation.4 | custom fusion | flops 1966080 | bytes 23593344 | tf_op jit(solution)/shard_map/scatter-add | solution.py:71
  675.6 4.4 convert_element_type.46
  680.1 14.4 %fusion.4 = bf16[24,16,128,128]{3,2,1,0:T(8,128)(2,1)} fusion(bf16[160,24,128,1]{2,0,3,1:T(8,128)(2,1)S(1)} %fusion.14, bf16[24,16,160,128]{3,2,1,0:T(8,128)(2,1)} %bitcast.65, pred[24,16]{1,0:T(8,128)(4,1)S(1)} %get-tuple-element.28), kind=kOutput, calls=%fused_computation.13 | convolution fusion | flops 2027421696 | bytes 29294976 | tf_op jit(solution)/shard_map/lsdc,dle->lsce/dot_general | solution.py:61
  694.4 52.6 %all-reduce.3.cloned.1.call-done = bf16[64,160,128]{2,1,0:T(8,128)(2,1)} async-done(((bf16[64,160,128]{2,1,0:T(8,128)(2,1)}), bf16[64,160,128]{2,1,0:T(8,128)(2,1)}) %all-reduce.3.cloned.1.call-update) | async-done | bytes 2621456 | tf_op jit(solution)/shard_map/psum | solution.py:76
  747.0 5.2 fusion.13
  752.2 4.1 copy.36
  (28 shorter events, 0.3 us)
Async XLA Ops:
  7.2 1.6 copy-start
  7.2 367.3 %all-gather.3.cloned.1.call-start = ((), (), s32[]{:S(2)}) async-start(), calls=%async_computation.3 | async-start | bytes 47185920 | tf_op jit(solution)/shard_map/all_gather | solution.py:16
  405.5 50.1 %all-to-all-start = ((bf16[4,24,160,128]{3,2,1,0:T(8,128)(2,1)}), bf16[4,24,160,128]{3,2,1,0:T(8,128)(2,1)}, u32[]{:S(2)}, u32[]{:S(2)}) async-start(bf16[4,24,160,128]{3,2,1,0:T(8,128)(2,1)} %broadcast_select_fusion.5), calls=%async_computation | async-start | bytes 7864320 | tf_op jit(solution)/shard_map/all_to_all | solution.py:45
  412.2 3.1 copy-start.3
  594.5 49.3 %all-to-all-start.1 = ((bf16[4,24,160,128]{3,2,1,0:T(8,128)(2,1)}), bf16[4,24,160,128]{3,2,1,0:T(8,128)(2,1)}, u32[]{:S(2)}, u32[]{:S(2)}) async-start(bf16[4,24,160,128]{3,2,1,0:T(8,128)(2,1)} %bitcast.66), calls=%async_computation.1 | async-start | bytes 7864320 | tf_op jit(solution)/shard_map/all_to_all | solution.py:70
  599.3 147.7 %all-reduce.3.cloned.1.call-start = ((), (), s32[]{:S(2)}) async-start(), calls=%async_computation.2 | async-start | bytes 5242880 | tf_op jit(solution)/shard_map/psum | solution.py:76
  680.0 67.0 %copy-start.2 = (bf16[160,128]{1,0:T(8,128)(2,1)S(1)}, bf16[160,128]{1,0:T(8,128)(2,1)}, u32[]{:S(2)}) copy-start(bf16[160,128]{1,0:T(8,128)(2,1)} %param.5) | copy-start | bytes 122884
  680.0 76.2 %copy-start.1 = (bf16[128,8192]{1,0:T(8,128)(2,1)S(1)}, bf16[128,8192]{1,0:T(8,128)(2,1)}, u32[]{:S(2)}) copy-start(bf16[128,8192]{1,0:T(8,128)(2,1)} %param.6) | copy-start | bytes 6291460
Sparse Core Ops, SparseCore 0:
  12.9 361.5 all-gather.2
  680.2 66.8 all-reduce.2
